TPU v7x, 32 devices: a whole 2x2x4 slice. The times are simulated.
32 devices in a mesh: elem: 8 (over z, core), front: 4 (over y, x).
Axes of the slice: x: 2, y: 2, z: 4, core: 2. Of those that a mesh axis runs over, the one named last changes fastest.
Arguments:
- elem_mat: bfloat16 [24, 24, 4096], P(None, None, ('elem', 'front')), may hold values from -1.25 to 1.25
- elem_deriv: bfloat16 [24, 24, 4096], P(None, None, ('elem', 'front')), may hold values from -1.1953125 to 1.1953125
- elem_disp: bfloat16 [24, 4096], P(None, ('elem', 'front')), may hold values from -6 to 6
- elem_sens: bfloat16 [4096, 24, 512], P(('elem', 'front')), may hold values from -3 to 3
- design_var: int32 [4096], P(('elem', 'front')), may hold values from 0 to 511
- dof_rows: int32 [24, 4096], P(None, ('elem', 'front')), may hold values from 0 to 14336, as said below
- inverse_factor: bfloat16 [57344, 8192], P('front', 'elem'), may hold values from -2 to 2
- coupling: bfloat16 [8192, 49152], P('elem', 'front'), may hold values from -0.0625 to 0.0625
- front_sizes: int32 [7], replicated, may hold values from 4096 to 8192
Outputs:
- sens: float32 [57344, 512], P('front', 'elem')
Inputs may be any that keep to these rules, and one draw needn't show every extreme that they name: `dof_rows`: the used rows of one element lie in one aligned block of 128 rows; the value 14336 marks a degree of freedom that no front holds.
All inputs are finite; a program needn't handle non-finite values.
Results may differ from a plain program's by a relative error of at most 0.014.
Values may be sent and summed in bfloat16 or wider, within the bound.
A program may use at most 128 MiB of HBM per device.

v0:
```python
import jax
import jax.numpy as jnp
from jax import lax
from jax.sharding import PartitionSpec as P

FS = 8192
LEVELS = 3


def swapped(array, axis, bit):
    return lax.ppermute(array, axis, [(i, i ^ 1 << bit) for i in range(lax.axis_size(axis))])


def form_loads(tables, derivs, disps, sens_block, variables, places, column_base, spot_rows):
    column_count = sens_block.shape[2]
    pseudo = -jnp.einsum("ije,ejc->eic", tables, sens_block, preferred_element_type=jnp.float32)
    drive_term = -jnp.einsum("ije,je->ei", derivs, disps, preferred_element_type=jnp.float32)
    column_ids = column_base + lax.iota(jnp.int32, column_count)
    hit_column = (column_ids[None, :] == variables[:, None]).astype(jnp.float32)
    pseudo = pseudo + drive_term[:, :, None] * hit_column[:, None, :]
    term_rows = jnp.zeros((spot_rows, column_count), jnp.float32)
    return term_rows.at[places.T.reshape(-1)].add(pseudo.reshape(-1, column_count), mode="drop")


def gather_group(local_block, bit_count, device):
    if bit_count == 0:
        return local_block
    for bit_at in range(bit_count):
        partner = swapped(local_block, "front", bit_at)
        is_upper = device >> bit_at & 1 == 1
        local_block = jnp.where(
            is_upper,
            jnp.concatenate([partner, local_block], 0),
            jnp.concatenate([local_block, partner], 0),
        )
    return local_block


def reduce_group(partial_value, bit_count, device):
    if bit_count == 0:
        return partial_value
    for bit_at in reversed(range(bit_count)):
        half_rows = partial_value.shape[0] // 2
        lower_half = partial_value[:half_rows]
        upper_half = partial_value[half_rows:]
        is_upper = device >> bit_at & 1 == 1
        kept_half = jnp.where(is_upper, upper_half, lower_half)
        sent_half = jnp.where(is_upper, lower_half, upper_half)
        partial_value = kept_half + swapped(sent_half, "front", bit_at)
    return partial_value


def to_row_block(local_block, bit_count, device):
    whole_front = gather_group(local_block, bit_count, device)
    return lax.all_to_all(whole_front, "elem", split_axis=0, concat_axis=1, tiled=True)


def from_row_block(partial_value, bit_count, device):
    spread = lax.all_to_all(partial_value, "elem", split_axis=1, concat_axis=0, tiled=True)
    return reduce_group(spread, bit_count, device)


def body(
    elem_mat,
    elem_deriv,
    elem_disp,
    elem_sens,
    design_var,
    dof_rows,
    inverse_factor,
    coupling,
    front_sizes,
):
    front_count = lax.axis_size("front")
    depth_bits = front_count.bit_length() - 1
    device = lax.axis_index("front")
    spot_rows = inverse_factor.shape[0]
    own_sens = lax.all_to_all(elem_sens, "elem", split_axis=2, concat_axis=0, tiled=True)
    tables, derivs, disps = (
        lax.all_gather(elem_mat, "elem", axis=2, tiled=True),
        lax.all_gather(elem_deriv, "elem", axis=2, tiled=True),
        lax.all_gather(elem_disp, "elem", axis=1, tiled=True),
    )
    variables, places = (
        lax.all_gather(design_var, "elem", axis=0, tiled=True),
        lax.all_gather(dof_rows, "elem", axis=1, tiled=True),
    )
    column_base = lax.axis_index("elem") * own_sens.shape[2]
    load_rows = form_loads(
        tables, derivs, disps, own_sens, variables, places, column_base, spot_rows
    )
    level_facts = []
    offset = 0
    first_front = 0
    for level_at in range(LEVELS):
        bit_count = depth_bits - (LEVELS - 1 - level_at)
        block_rows = FS >> bit_count
        front_id = first_front + (device >> bit_count)
        size_now = lax.dynamic_index_in_dim(front_sizes, front_id, 0, keepdims=False)
        rows_at = (device & (1 << bit_count) - 1) * block_rows + lax.iota(jnp.int32, block_rows)
        live_rows = (rows_at < size_now).astype(jnp.float32)[:, None]
        level_facts.append((bit_count, block_rows, offset, live_rows))
        offset = offset + block_rows
        first_front = first_front + (1 << LEVELS - 1 - level_at)
    forward_out = []
    acc_rows = None
    for level_at in range(LEVELS):
        bit_count, block_rows, offset, live_rows = level_facts[level_at]
        given = load_rows[offset : offset + block_rows]
        if acc_rows is not None:
            given = given - acc_rows
        rhs_in = (live_rows * given).astype(jnp.bfloat16)
        rhs_rows = to_row_block(rhs_in, bit_count, device)
        factor_rows = inverse_factor[offset : offset + block_rows]
        partial_value = jnp.dot(factor_rows, rhs_rows, preferred_element_type=jnp.float32)
        solved = live_rows * lax.psum_scatter(
            partial_value, "elem", scatter_dimension=1, tiled=True
        )
        forward_out.append(solved)
        if level_at < LEVELS - 1:
            wide_solved = lax.all_gather(solved.astype(jnp.bfloat16), "elem", axis=1, tiled=True)
            links = coupling[:, offset : offset + block_rows]
            parent_part = jnp.dot(links, wide_solved, preferred_element_type=jnp.float32)
            acc_rows = from_row_block(parent_part, bit_count + 1, device)
    pieces_out = [None] * LEVELS
    parent_rows = None
    for level_at in reversed(range(LEVELS)):
        bit_count, block_rows, offset, live_rows = level_facts[level_at]
        residual = forward_out[level_at]
        if parent_rows is not None:
            parent_block = to_row_block(parent_rows, bit_count + 1, device)
            links = coupling[:, offset : offset + block_rows]
            correction = lax.dot_general(
                links, parent_block, (((0,), (0,)), ((), ())), preferred_element_type=jnp.float32
            )
            residual = residual - lax.psum_scatter(
                correction, "elem", scatter_dimension=1, tiled=True
            )
        back_in = (live_rows * residual).astype(jnp.bfloat16)
        wide_back = lax.all_gather(back_in, "elem", axis=1, tiled=True)
        factor_rows = inverse_factor[offset : offset + block_rows]
        partial_value = lax.dot_general(
            factor_rows, wide_back, (((0,), (0,)), ((), ())), preferred_element_type=jnp.float32
        )
        answer = live_rows * from_row_block(partial_value, bit_count, device)
        pieces_out[level_at] = answer
        parent_rows = answer.astype(jnp.bfloat16)
    return jnp.concatenate(pieces_out, 0)


def solution(mesh):
    return jax.shard_map(
        body,
        mesh=mesh,
        in_specs=(
            P(None, None, ("elem", "front")),
            P(None, None, ("elem", "front")),
            P(None, ("elem", "front")),
            P(("elem", "front"), None, None),
            P(("elem", "front")),
            P(None, ("elem", "front")),
            P("front", "elem"),
            P("elem", "front"),
            P(),
        ),
        out_specs=P("front", "elem"),
        check_vma=False,
    )
```

profile of v0, /device:TPU:0, one launch (start us, length us, event | category | flops | bytes accessed | tf_op | source)
XLA Modules:
  0.0 1891.1 jit_solution(9125538343845212889)
XLA Ops:
  19.9 95.3 %all_gather.30 = s32[24,1024]{1,0:T(8,128)S(1)} all-gather(s32[24,128]{1,0:T(8,128)S(1)} %copy-done.3), channel_id=1, replica_groups=mesh['elem'=8,'front'=4] {'elem'}, dimensions={1}, use_global_device_ids=true | all-gather | bytes 110592 | tf_op jit(solution)/shard_map/all_gather | solution.py:86
  118.3 11.1 all-gather
  129.5 12.7 all_gather.33
  171.0 134.3 %scatter_custom_fusion = f32[14336,64]{1,0:T(8,128)} fusion(s32[24576]{0:T(1024)S(1)} %bitcast.156, f32[24576,64]{1,0:T(8,128)} %bitcast.120, f32[]{:T(128)} %constant.14.clone.1), kind=kCustom, calls=%fused_computation.27 | custom fusion | flops 1572864 | bytes 3670528 | tf_op jit(solution)/shard_map/scatter-add | solution.py:22
  312.7 29.4 %all_to_all.184 = bf16[8,1024,64]{1,2,0:T(8,128)(2,1)S(1)} all-to-all(bf16[8,1024,64]{1,2,0:T(8,128)(2,1)S(1)} %bitcast.137), channel_id=1, replica_groups=mesh['elem'=8,'front'=4] {'elem'}, dimensions={0} | all-to-all | bytes 2097152 | tf_op jit(solution)/shard_map/all_to_all | solution.py:55
  342.2 15.8 fusion.8
  358.1 167.1 %reduce-scatter.6.cloned.1.call-done = f32[8192,64]{0,1:T(8,128)} async-done(((f32[8192,512]{0,1:T(8,128)}), f32[8192,64]{0,1:T(8,128)}) %reduce-scatter.6.cloned.1.call-update) | async-done | bytes 2097168 | tf_op jit(solution)/shard_map/reduce_scatter | solution.py:116
  527.9 80.7 %all-gather.13.cloned.1.call-done = bf16[8192,512]{0,1:T(8,128)(2,1)} async-done(((bf16[8192,64]{0,1:T(8,128)(2,1)}), bf16[8192,512]{0,1:T(8,128)(2,1)}) %all-gather.13.cloned.1.call-update) | async-done | bytes 8388624 | tf_op jit(solution)/shard_map/all_gather | solution.py:121
  608.6 15.8 fusion.2
  628.1 48.9 %all-to-all-done.2 = f32[1024,8,64]{0,2,1:T(8,128)S(1)} async-done(((f32[1024,8,64]{0,2,1:T(8,128)}), f32[1024,8,64]{0,2,1:T(8,128)S(1)}, u32[]{:S(2)}, u32[]{:S(2)}) %all-to-all-start.2) | async-done | bytes 2097184 | tf_op jit(solution)/shard_map/all_to_all | solution.py:59
  683.2 21.0 %collective-permute-done = f32[4096,64]{0,1:T(8,128)} collective-permute-done((f32[4096,64]{0,1:T(8,128)}, f32[4096,64]{0,1:T(8,128)}, u32[]{:S(2)}, u32[]{:S(2)}) %collective-permute-start) | collective-permute-done | bytes 1048608 | tf_op jit(solution)/shard_map/ppermute | solution.py:11
  718.5 29.9 %all_to_all.185 = bf16[8,1024,64]{1,2,0:T(8,128)(2,1)S(1)} all-to-all(bf16[8,1024,64]{1,2,0:T(8,128)(2,1)S(1)} %bitcast.138), channel_id=1, replica_groups=mesh['elem'=8,'front'=4] {'elem'}, dimensions={0} | all-to-all | bytes 2097152 | tf_op jit(solution)/shard_map/all_to_all | solution.py:55
  758.8 88.3 %reduce-scatter.8.cloned.1.call-done = f32[4096,64]{0,1:T(8,128)} async-done(((f32[4096,512]{0,1:T(8,128)}), f32[4096,64]{0,1:T(8,128)}) %reduce-scatter.8.cloned.1.call-update) | async-done | bytes 1048592 | tf_op jit(solution)/shard_map/reduce_scatter | solution.py:116
  849.3 45.5 %all-gather.15.cloned.1.call-done = bf16[4096,512]{0,1:T(8,128)(2,1)} async-done(((bf16[4096,64]{0,1:T(8,128)(2,1)}), bf16[4096,512]{0,1:T(8,128)(2,1)}) %all-gather.15.cloned.1.call-update) | async-done | bytes 4194320 | tf_op jit(solution)/shard_map/all_gather | solution.py:121
  908.9 48.9 %all-to-all-done.4 = f32[1024,8,64]{0,2,1:T(8,128)S(1)} async-done(((f32[1024,8,64]{0,2,1:T(8,128)}), f32[1024,8,64]{0,2,1:T(8,128)S(1)}, u32[]{:S(2)}, u32[]{:S(2)}) %all-to-all-start.4) | async-done | bytes 2097184 | tf_op jit(solution)/shard_map/all_to_all | solution.py:59
  959.8 23.0 %collective-permute-done.2 = f32[4096,64]{0,1:T(8,128)S(1)} collective-permute-done((f32[4096,64]{0,1:T(8,128)S(1)}, f32[4096,64]{0,1:T(8,128)S(1)}, u32[]{:S(2)}, u32[]{:S(2)}) %collective-permute-start.2) | collective-permute-done | bytes 1048608 | tf_op jit(solution)/shard_map/ppermute | solution.py:11
  1014.3 30.9 %all_to_all.186 = bf16[8,1024,64]{1,2,0:T(8,128)(2,1)S(1)} all-to-all(bf16[8,1024,64]{1,2,0:T(8,128)(2,1)S(1)} %bitcast.139), channel_id=1, replica_groups=mesh['elem'=8,'front'=4] {'elem'}, dimensions={0} | all-to-all | bytes 2097152 | tf_op jit(solution)/shard_map/all_to_all | solution.py:55
  1051.9 48.9 %reduce-scatter.10.cloned.1.call-done = f32[2048,64]{0,1:T(8,128)} async-done(((f32[2048,512]{0,1:T(8,128)}), f32[2048,64]{0,1:T(8,128)}) %reduce-scatter.10.cloned.1.call-update) | async-done | bytes 524304 | tf_op jit(solution)/shard_map/reduce_scatter | solution.py:116
  1102.6 27.7 %all-gather.17.cloned.1.call-done = bf16[2048,512]{0,1:T(8,128)(2,1)} async-done(((bf16[2048,64]{0,1:T(8,128)(2,1)}), bf16[2048,512]{0,1:T(8,128)(2,1)}) %all-gather.17.cloned.1.call-update) | async-done | bytes 2097168 | tf_op jit(solution)/shard_map/all_gather | solution.py:140
  1135.5 51.9 %all_to_all.187 = f32[1024,8,64]{0,2,1:T(8,128)S(1)} all-to-all(f32[1024,8,64]{0,2,1:T(8,128)S(1)} %bitcast.144), channel_id=1, replica_groups=mesh['elem'=8,'front'=4] {'elem'}, dimensions={1} | all-to-all | bytes 4194304 | tf_op jit(solution)/shard_map/all_to_all | solution.py:59
  1189.5 23.0 %collective-permute-done.6 = f32[4096,64]{0,1:T(8,128)S(1)} collective-permute-done((f32[4096,64]{0,1:T(8,128)S(1)}, f32[4096,64]{0,1:T(8,128)S(1)}, u32[]{:S(2)}, u32[]{:S(2)}) %collective-permute-start.6) | collective-permute-done | bytes 1048608 | tf_op jit(solution)/shard_map/ppermute | solution.py:11
  1243.3 31.4 %all_to_all.188 = bf16[8,1024,64]{1,2,0:T(8,128)(2,1)S(1)} all-to-all(bf16[8,1024,64]{1,2,0:T(8,128)(2,1)S(1)} %bitcast.140), channel_id=1, replica_groups=mesh['elem'=8,'front'=4] {'elem'}, dimensions={0} | all-to-all | bytes 2097152 | tf_op jit(solution)/shard_map/all_to_all | solution.py:55
  1284.9 88.5 %reduce-scatter.12.cloned.1.call-done = f32[4096,64]{0,1:T(8,128)} async-done(((f32[4096,512]{0,1:T(8,128)}), f32[4096,64]{0,1:T(8,128)}) %reduce-scatter.12.cloned.1.call-update) | async-done | bytes 1048592 | tf_op jit(solution)/shard_map/reduce_scatter | solution.py:136
  1375.6 45.4 %all-gather.19.cloned.1.call-done = bf16[4096,512]{0,1:T(8,128)(2,1)} async-done(((bf16[4096,64]{0,1:T(8,128)(2,1)}), bf16[4096,512]{0,1:T(8,128)(2,1)}) %all-gather.19.cloned.1.call-update) | async-done | bytes 4194320 | tf_op jit(solution)/shard_map/all_gather | solution.py:140
  1429.2 51.5 %all_to_all.189 = f32[1024,8,64]{0,2,1:T(8,128)S(1)} all-to-all(f32[1024,8,64]{0,2,1:T(8,128)S(1)} %bitcast.145), channel_id=1, replica_groups=mesh['elem'=8,'front'=4] {'elem'}, dimensions={1} | all-to-all | bytes 4194304 | tf_op jit(solution)/shard_map/all_to_all | solution.py:59
  1482.7 23.0 %collective-permute-done.10 = f32[4096,64]{0,1:T(8,128)S(1)} collective-permute-done((f32[4096,64]{0,1:T(8,128)S(1)}, f32[4096,64]{0,1:T(8,128)S(1)}, u32[]{:S(2)}, u32[]{:S(2)}) %collective-permute-start.10) | collective-permute-done | bytes 1048608 | tf_op jit(solution)/shard_map/ppermute | solution.py:11
  1518.7 30.1 %all_to_all.190 = bf16[8,1024,64]{1,2,0:T(8,128)(2,1)S(1)} all-to-all(bf16[8,1024,64]{1,2,0:T(8,128)(2,1)S(1)} %bitcast.141), channel_id=1, replica_groups=mesh['elem'=8,'front'=4] {'elem'}, dimensions={0} | all-to-all | bytes 2097152 | tf_op jit(solution)/shard_map/all_to_all | solution.py:55
  1548.8 15.7 fusion.11
  1564.6 167.1 %reduce-scatter.14.cloned.1.call-done = f32[8192,64]{0,1:T(8,128)} async-done(((f32[8192,512]{0,1:T(8,128)}), f32[8192,64]{0,1:T(8,128)}) %reduce-scatter.14.cloned.1.call-update) | async-done | bytes 2097168 | tf_op jit(solution)/shard_map/reduce_scatter | solution.py:136
  1734.5 80.6 %all-gather.21.cloned.1.call-done = bf16[8192,512]{0,1:T(8,128)(2,1)} async-done(((bf16[8192,64]{0,1:T(8,128)(2,1)}), bf16[8192,512]{0,1:T(8,128)(2,1)}) %all-gather.21.cloned.1.call-update) | async-done | bytes 8388624 | tf_op jit(solution)/shard_map/all_gather | solution.py:140
  1815.2 14.3 fusion.4
  1829.4 51.5 %all_to_all.191 = f32[1024,8,64]{0,2,1:T(8,128)S(1)} all-to-all(f32[1024,8,64]{0,2,1:T(8,128)S(1)} %bitcast.146), channel_id=1, replica_groups=mesh['elem'=8,'front'=4] {'elem'}, dimensions={1} | all-to-all | bytes 4194304 | tf_op jit(solution)/shard_map/all_to_all | solution.py:59
  (135 shorter events, 227.5 us)
Async XLA Ops:
  6.5 137.2 %all-gather.11.cloned.1.call-start = ((), (), s32[]{:S(2)}) async-start(), calls=%async_computation.17 | async-start | bytes 1327104 | tf_op jit(solution)/shard_map/all_gather | solution.py:81
  12.6 105.1 %copy-start.5 = (s32[7]{0:T(128)S(1)}, s32[7]{0:T(128)}, u32[]{:S(2)}) copy-start(s32[7]{0:T(128)} %param.17) | copy-start | bytes 88
  12.6 105.7 %copy-start.6 = (s32[128]{0:T(128)S(1)}, s32[128]{0:T(128)}, u32[]{:S(2)}) copy-start(s32[128]{0:T(128)} %param.13) | copy-start | bytes 1540
  12.6 116.9 %copy-start.4 = (bf16[24,128]{1,0:T(8,128)(2,1)S(1)}, bf16[24,128]{1,0:T(8,128)(2,1)}, u32[]{:S(2)}) copy-start(bf16[24,128]{1,0:T(8,128)(2,1)} %param.11) | copy-start | bytes 18436
  12.6 143.2 %all-to-all-start = ((bf16[128,24,512]{0,1,2:T(8,128)(2,1)}), bf16[128,24,512]{0,1,2:T(8,128)(2,1)S(1)}, u32[]{:S(2)}, u32[]{:S(2)}) async-start(bf16[128,24,512]{0,1,2:T(8,128)(2,1)} %copy.36), calls=%async_computation | async-start | bytes 6291456 | tf_op jit(solution)/shard_map/all_to_all | solution.py:78
  19.1 129.2 %all-gather.9.cloned.1.call-start = ((), (), s32[]{:S(2)}) async-start(), calls=%async_computation.16 | async-start | bytes 1327104 | tf_op jit(solution)/shard_map/all_gather | solution.py:80
  19.9 505.4 %reduce-scatter.6.cloned.1.call-start = ((), (), s32[]{:S(2)}) async-start(), calls=%async_computation.18 | async-start | bytes 18874368 | tf_op jit(solution)/shard_map/reduce_scatter | solution.py:116
  358.1 250.5 %all-gather.13.cloned.1.call-start = ((), (), s32[]{:S(2)}) async-start(), calls=%async_computation.19 | async-start | bytes 9437184 | tf_op jit(solution)/shard_map/all_gather | solution.py:121
  624.4 52.6 %all-to-all-start.2 = ((f32[1024,8,64]{0,2,1:T(8,128)}), f32[1024,8,64]{0,2,1:T(8,128)S(1)}, u32[]{:S(2)}, u32[]{:S(2)}) async-start(f32[1024,8,64]{0,2,1:T(8,128)} %bitcast.143), calls=%async_computation.3 | async-start | bytes 4194304 | tf_op jit(solution)/shard_map/all_to_all | solution.py:59
  628.0 219.1 %reduce-scatter.8.cloned.1.call-start = ((), (), s32[]{:S(2)}) async-start(), calls=%async_computation.20 | async-start | bytes 9437184 | tf_op jit(solution)/shard_map/reduce_scatter | solution.py:116
  679.2 24.9 %collective-permute-start = (f32[4096,64]{0,1:T(8,128)}, f32[4096,64]{0,1:T(8,128)}, u32[]{:S(2)}, u32[]{:S(2)}) collective-permute-start(f32[4096,64]{0,1:T(8,128)} %bitcast.67), channel_id=1, source_target_pairs={{0,1},{1,0},{2,3},{3,2},{4,5},{5,4},{6,7},{7,6},{8,9},{9,8},{10,11... | collective-permute-start | bytes 3145736 | tf_op jit(solution)/shard_map/ppermute | solution.py:11
  705.6 12.6 collective-permute-start.1
  758.6 136.1 %all-gather.15.cloned.1.call-start = ((), (), s32[]{:S(2)}) async-start(), calls=%async_computation.21 | async-start | bytes 4718592 | tf_op jit(solution)/shard_map/all_gather | solution.py:121
  905.2 52.6 %all-to-all-start.4 = ((f32[1024,8,64]{0,2,1:T(8,128)}), f32[1024,8,64]{0,2,1:T(8,128)S(1)}, u32[]{:S(2)}, u32[]{:S(2)}) async-start(f32[1024,8,64]{0,2,1:T(8,128)} %bitcast.142), calls=%async_computation.6 | async-start | bytes 4194304 | tf_op jit(solution)/shard_map/all_to_all | solution.py:59
  908.9 191.9 %reduce-scatter.10.cloned.1.call-start = ((), (), s32[]{:S(2)}) async-start(), calls=%async_computation.22 | async-start | bytes 4718592 | tf_op jit(solution)/shard_map/reduce_scatter | solution.py:116
  958.2 24.7 %collective-permute-start.2 = (f32[4096,64]{0,1:T(8,128)S(1)}, f32[4096,64]{0,1:T(8,128)S(1)}, u32[]{:S(2)}, u32[]{:S(2)}) collective-permute-start(f32[4096,64]{0,1:T(8,128)S(1)} %bitcast.147), channel_id=1, source_target_pairs={{0,2},{1,3},{2,0},{3,1},{4,6},{5,7},{6,4},{7,5},{8,10},{9,11},{10,... | collective-permute-start | bytes 3145736 | tf_op jit(solution)/shard_map/ppermute | solution.py:11
  983.0 12.7 collective-permute-start.3
  996.9 6.4 collective-permute-start.4
  1003.4 10.6 collective-permute-start.5
  1051.8 78.5 %all-gather.17.cloned.1.call-start = ((), (), s32[]{:S(2)}) async-start(), calls=%async_computation.23 | async-start | bytes 2359296 | tf_op jit(solution)/shard_map/all_gather | solution.py:140
  1102.6 270.8 %reduce-scatter.12.cloned.1.call-start = ((), (), s32[]{:S(2)}) async-start(), calls=%async_computation.24 | async-start | bytes 9437184 | tf_op jit(solution)/shard_map/reduce_scatter | solution.py:136
  1187.8 24.6 %collective-permute-start.6 = (f32[4096,64]{0,1:T(8,128)S(1)}, f32[4096,64]{0,1:T(8,128)S(1)}, u32[]{:S(2)}, u32[]{:S(2)}) collective-permute-start(f32[4096,64]{0,1:T(8,128)S(1)} %bitcast.148), channel_id=1, source_target_pairs={{0,2},{1,3},{2,0},{3,1},{4,6},{5,7},{6,4},{7,5},{8,10},{9,11},{10,... | collective-permute-start | bytes 3145736 | tf_op jit(solution)/shard_map/ppermute | solution.py:11
  1212.6 12.5 collective-permute-start.7
  1226.0 6.4 collective-permute-start.8
  1232.5 10.5 collective-permute-start.9
  1284.8 88.6 %copy-start.1 = (f32[4096,64]{0,1:T(8,128)S(1)}, f32[4096,64]{0,1:T(8,128)}, u32[]{:S(2)}) copy-start(f32[4096,64]{0,1:T(8,128)} %reduce-scatter.8.cloned.1.call-done) | copy-start | bytes 3145732
  1284.9 136.2 %all-gather.19.cloned.1.call-start = ((), (), s32[]{:S(2)}) async-start(), calls=%async_computation.25 | async-start | bytes 4718592 | tf_op jit(solution)/shard_map/all_gather | solution.py:140
  1375.6 356.1 %reduce-scatter.14.cloned.1.call-start = ((), (), s32[]{:S(2)}) async-start(), calls=%async_computation.26 | async-start | bytes 18874368 | tf_op jit(solution)/shard_map/reduce_scatter | solution.py:136
  1481.1 24.6 %collective-permute-start.10 = (f32[4096,64]{0,1:T(8,128)S(1)}, f32[4096,64]{0,1:T(8,128)S(1)}, u32[]{:S(2)}, u32[]{:S(2)}) collective-permute-start(f32[4096,64]{0,1:T(8,128)S(1)} %bitcast.149), channel_id=1, source_target_pairs={{0,1},{1,0},{2,3},{3,2},{4,5},{5,4},{6,7},{7,6},{8,9},{9,8},{10,11... | collective-permute-start | bytes 3145736 | tf_op jit(solution)/shard_map/ppermute | solution.py:11
  1505.9 12.5 collective-permute-start.11
  1564.5 167.2 %copy-start = (f32[8192,64]{0,1:T(8,128)S(1)}, f32[8192,64]{0,1:T(8,128)}, u32[]{:S(2)}) copy-start(f32[8192,64]{0,1:T(8,128)} %reduce-scatter.6.cloned.1.call-done) | copy-start | bytes 6291460
  1564.5 250.6 %all-gather.21.cloned.1.call-start = ((), (), s32[]{:S(2)}) async-start(), calls=%async_computation.27 | async-start | bytes 9437184 | tf_op jit(solution)/shard_map/all_gather | solution.py:140
  (4 other events, 36.9 us)
Sparse Core Ops, SparseCore 0:
  8.9 42.0 all-gather.10
  52.6 45.5 all-gather.8
  358.2 167.0 reduce-scatter.5
  528.1 80.4 all-gather.12
  758.7 88.3 reduce-scatter.7
  849.4 45.3 all-gather.14
  1051.9 48.7 reduce-scatter.9
  1102.7 27.6 all-gather.16
  1285.0 88.3 reduce-scatter.11
  1375.7 45.3 all-gather.18
  1564.6 167.0 reduce-scatter.13
  1734.6 80.4 all-gather.20
where the time goes:
time: 1900 us; the launch traced here: 1890 us
  waiting for transfers between devices  1100 us (58%)
  blocking collectives  426 us (22%)
  other arithmetic  162 us (9%)
  matrix products  122 us (6%)
  local copies, waits for them, and re-layouts  35 us (2%)
  starting transfers between devices  32.6 us (2%)
    reduce_scatter x3, waiting for transfers between devices, body(): lax.psum_scatter(partial_value, 'elem', scatter_dimension=1, tiled=True)  304 us
    reduce_scatter x2, waiting for transfers between devices, body(): lax.psum_scatter(correction, 'elem', scatter_dimension=1, tiled=True)  256 us
    ppermute x12, waiting for transfers between devices, swapped(): lax.ppermute(array, axis, [(i, i ^ 1 << bit) for i in range(lax.axis_size...  161 us
    all_to_all x3, blocking collectives, from_row_block(): lax.all_to_all(partial_value, 'elem', split_axis=1, concat_axis=0, tiled=...  155 us
    all_gather x3, waiting for transfers between devices, body(): wide_back = lax.all_gather(back_in, 'elem', axis=1, tiled=True)  154 us
    all_to_all x5, blocking collectives, to_row_block(): lax.all_to_all(whole_front, 'elem', split_axis=0, concat_axis=1, tiled=True)  152 us
    scatter-add x1, other arithmetic, form_loads(): term_rows.at[places.T.reshape(-1)]  134 us
    all_gather x2, waiting for transfers between devices, body(): lax.all_gather(solved.astype(jnp.bfloat16), 'elem', axis=1, tiled=True)  126 us
  transfers between devices with their start and end apart: 27, of which 24 were waited for; matrix products, arithmetic and copies ran while one was open for 1% of the time, Pallas kernels for 0%

commit v1 on v0

--- a/solution.py
+++ b/solution.py
@@ -137,7 +137,15 @@
                 correction, "elem", scatter_dimension=1, tiled=True
             )
         back_in = (live_rows * residual).astype(jnp.bfloat16)
-        wide_back = lax.all_gather(back_in, "elem", axis=1, tiled=True)
+        n_dev = lax.axis_size("elem")
+        moving, blocks = (back_in, [back_in])
+        for _ in range(n_dev - 1):
+            moving = lax.ppermute(
+                moving, "elem", [(i_2, (i_2 + 1) % n_dev) for i_2 in range(n_dev)]
+            )
+            blocks.insert(0, moving)
+        line = jnp.concatenate(blocks, axis=1)
+        wide_back = jnp.roll(line, (lax.axis_index("elem") + 1) * back_in.shape[1], axis=1)
         factor_rows = inverse_factor[offset : offset + block_rows]
         partial_value = lax.dot_general(
             factor_rows, wide_back, (((0,), (0,)), ((), ())), preferred_element_type=jnp.float32

time: 1900 us -> 2000 us (1.053)
  waiting for transfers between devices: 1100 us -> 1180 us
    ppermute x0 -> x21, waiting for transfers between devices: none -> 238 us  [body(): lax.ppermute(moving, 'elem', [(i_2, (i_2 + 1) % n_dev) for i_2 in range(n...]
    all_gather x3 -> x0, waiting for transfers between devices: 154 us -> none  [body(): wide_back = lax.all_gather(back_in, 'elem', axis=1, tiled=True)]
  transfers between devices with their start and end apart: 27 -> 45, of which waited for: 24 -> 42; matrix products, arithmetic and copies ran while one was open for 1% -> 1% of each run, Pallas kernels for 0% -> 0%
where the time goes in v1:
time: 2000 us; the launch traced here: 1990 us
  waiting for transfers between devices  1180 us (59%)
  blocking collectives  426 us (21%)
  other arithmetic  162 us (8%)
  matrix products  120 us (6%)
  local copies, waits for them, and re-layouts  52.5 us (3%)
  starting transfers between devices  33.6 us (2%)
    reduce_scatter x3, waiting for transfers between devices, body(): lax.psum_scatter(partial_value, 'elem', scatter_dimension=1, tiled=True)  304 us
    reduce_scatter x2, waiting for transfers between devices, body(): lax.psum_scatter(correction, 'elem', scatter_dimension=1, tiled=True)  256 us
    ppermute x21, waiting for transfers between devices, body(): lax.ppermute(moving, 'elem', [(i_2, (i_2 + 1) % n_dev) for i_2 in range(n...  238 us
    ppermute x12, waiting for transfers between devices, swapped(): lax.ppermute(array, axis, [(i, i ^ 1 << bit) for i in range(lax.axis_size...  161 us
    all_to_all x3, blocking collectives, from_row_block(): lax.all_to_all(partial_value, 'elem', split_axis=1, concat_axis=0, tiled=...  155 us
    all_to_all x5, blocking collectives, to_row_block(): lax.all_to_all(whole_front, 'elem', split_axis=0, concat_axis=1, tiled=True)  151 us
    scatter-add x1, other arithmetic, form_loads(): term_rows.at[places.T.reshape(-1)]  134 us
    all_gather x2, waiting for transfers between devices, body(): lax.all_gather(solved.astype(jnp.bfloat16), 'elem', axis=1, tiled=True)  126 us
  transfers between devices with their start and end apart: 45, of which 42 were waited for; matrix products, arithmetic and copies ran while one was open for 1% of the time, Pallas kernels for 0%

profile of v1, /device:TPU:0, one launch (start us, length us, event | category | flops | bytes accessed | tf_op | source)
XLA Modules:
  0.0 1992.2 jit_solution(9682564635656947044)
XLA Ops:
  19.8 95.4 %all_gather.21 = s32[24,1024]{1,0:T(8,128)S(1)} all-gather(s32[24,128]{1,0:T(8,128)S(1)} %copy-done.4), channel_id=1, replica_groups=mesh['elem'=8,'front'=4] {'elem'}, dimensions={1}, use_global_device_ids=true | all-gather | bytes 110592 | tf_op jit(solution)/shard_map/all_gather | solution.py:86
  171.2 134.3 %scatter_custom_fusion = f32[14336,64]{1,0:T(8,128)} fusion(s32[24576]{0:T(1024)S(1)} %bitcast.152, f32[24576,64]{1,0:T(8,128)} %bitcast.117, f32[]{:T(128)} %constant.69.clone.1), kind=kCustom, calls=%fused_computation.29 | custom fusion | flops 1572864 | bytes 3670528 | tf_op jit(solution)/shard_map/scatter-add | solution.py:22
  313.0 29.2 %all_to_all.184 = bf16[8,1024,64]{1,2,0:T(8,128)(2,1)S(1)} all-to-all(bf16[8,1024,64]{1,2,0:T(8,128)(2,1)S(1)} %bitcast.133), channel_id=1, replica_groups=mesh['elem'=8,'front'=4] {'elem'}, dimensions={0} | all-to-all | bytes 2097152 | tf_op jit(solution)/shard_map/all_to_all | solution.py:55
  342.2 15.8 fusion.8
  358.1 167.1 %reduce-scatter.6.cloned.1.call-done = f32[8192,64]{0,1:T(8,128)} async-done(((f32[8192,512]{0,1:T(8,128)}), f32[8192,64]{0,1:T(8,128)}) %reduce-scatter.6.cloned.1.call-update) | async-done | bytes 2097168 | tf_op jit(solution)/shard_map/reduce_scatter | solution.py:116
  527.9 80.7 %all-gather.10.cloned.1.call-done = bf16[8192,512]{0,1:T(8,128)(2,1)} async-done(((bf16[8192,64]{0,1:T(8,128)(2,1)}), bf16[8192,512]{0,1:T(8,128)(2,1)}) %all-gather.10.cloned.1.call-update) | async-done | bytes 8388624 | tf_op jit(solution)/shard_map/all_gather | solution.py:121
  608.5 15.8 fusion.2
  628.9 49.0 %all-to-all-done.2 = f32[1024,8,64]{0,2,1:T(8,128)} async-done(((f32[1024,8,64]{0,2,1:T(8,128)}), f32[1024,8,64]{0,2,1:T(8,128)}, u32[]{:S(2)}, u32[]{:S(2)}) %all-to-all-start.2) | async-done | bytes 2097184 | tf_op jit(solution)/shard_map/all_to_all | solution.py:59
  685.7 20.9 %collective-permute-done = f32[4096,64]{0,1:T(8,128)} collective-permute-done((f32[4096,64]{0,1:T(8,128)}, f32[4096,64]{0,1:T(8,128)}, u32[]{:S(2)}, u32[]{:S(2)}) %collective-permute-start) | collective-permute-done | bytes 1048608 | tf_op jit(solution)/shard_map/ppermute | solution.py:11
  721.0 29.9 %all_to_all.185 = bf16[8,1024,64]{1,2,0:T(8,128)(2,1)S(1)} all-to-all(bf16[8,1024,64]{1,2,0:T(8,128)(2,1)S(1)} %bitcast.134), channel_id=1, replica_groups=mesh['elem'=8,'front'=4] {'elem'}, dimensions={0} | all-to-all | bytes 2097152 | tf_op jit(solution)/shard_map/all_to_all | solution.py:55
  761.3 88.3 %reduce-scatter.8.cloned.1.call-done = f32[4096,64]{0,1:T(8,128)} async-done(((f32[4096,512]{0,1:T(8,128)}), f32[4096,64]{0,1:T(8,128)}) %reduce-scatter.8.cloned.1.call-update) | async-done | bytes 1048592 | tf_op jit(solution)/shard_map/reduce_scatter | solution.py:116
  851.7 45.5 %all-gather.12.cloned.1.call-done = bf16[4096,512]{0,1:T(8,128)(2,1)} async-done(((bf16[4096,64]{0,1:T(8,128)(2,1)}), bf16[4096,512]{0,1:T(8,128)(2,1)}) %all-gather.12.cloned.1.call-update) | async-done | bytes 4194320 | tf_op jit(solution)/shard_map/all_gather | solution.py:121
  911.4 48.9 %all-to-all-done.4 = f32[1024,8,64]{0,2,1:T(8,128)S(1)} async-done(((f32[1024,8,64]{0,2,1:T(8,128)}), f32[1024,8,64]{0,2,1:T(8,128)S(1)}, u32[]{:S(2)}, u32[]{:S(2)}) %all-to-all-start.4) | async-done | bytes 2097184 | tf_op jit(solution)/shard_map/all_to_all | solution.py:59
  962.3 23.0 %collective-permute-done.2 = f32[4096,64]{0,1:T(8,128)S(1)} collective-permute-done((f32[4096,64]{0,1:T(8,128)S(1)}, f32[4096,64]{0,1:T(8,128)S(1)}, u32[]{:S(2)}, u32[]{:S(2)}) %collective-permute-start.2) | collective-permute-done | bytes 1048608 | tf_op jit(solution)/shard_map/ppermute | solution.py:11
  1016.8 30.9 %all_to_all.186 = bf16[8,1024,64]{1,2,0:T(8,128)(2,1)S(1)} all-to-all(bf16[8,1024,64]{1,2,0:T(8,128)(2,1)S(1)} %bitcast.135), channel_id=1, replica_groups=mesh['elem'=8,'front'=4] {'elem'}, dimensions={0} | all-to-all | bytes 2097152 | tf_op jit(solution)/shard_map/all_to_all | solution.py:55
  1054.4 48.9 %reduce-scatter.10.cloned.1.call-done = f32[2048,64]{0,1:T(8,128)} async-done(((f32[2048,512]{0,1:T(8,128)}), f32[2048,64]{0,1:T(8,128)}) %reduce-scatter.10.cloned.1.call-update) | async-done | bytes 524304 | tf_op jit(solution)/shard_map/reduce_scatter | solution.py:116
  1163.7 51.9 %all_to_all.187 = f32[1024,8,64]{0,2,1:T(8,128)S(1)} all-to-all(f32[1024,8,64]{0,2,1:T(8,128)S(1)} %bitcast.141), channel_id=1, replica_groups=mesh['elem'=8,'front'=4] {'elem'}, dimensions={1} | all-to-all | bytes 4194304 | tf_op jit(solution)/shard_map/all_to_all | solution.py:59
  1217.7 22.9 %collective-permute-done.13 = f32[4096,64]{0,1:T(8,128)S(1)} collective-permute-done((f32[4096,64]{0,1:T(8,128)S(1)}, f32[4096,64]{0,1:T(8,128)S(1)}, u32[]{:S(2)}, u32[]{:S(2)}) %collective-permute-start.13) | collective-permute-done | bytes 1048608 | tf_op jit(solution)/shard_map/ppermute | solution.py:11
  1271.5 31.2 %all_to_all.188 = bf16[8,1024,64]{1,2,0:T(8,128)(2,1)S(1)} all-to-all(bf16[8,1024,64]{1,2,0:T(8,128)(2,1)S(1)} %bitcast.136), channel_id=1, replica_groups=mesh['elem'=8,'front'=4] {'elem'}, dimensions={0} | all-to-all | bytes 2097152 | tf_op jit(solution)/shard_map/all_to_all | solution.py:55
  1312.9 88.5 %reduce-scatter.12.cloned.1.call-done = f32[4096,64]{0,1:T(8,128)} async-done(((f32[4096,512]{0,1:T(8,128)}), f32[4096,64]{0,1:T(8,128)}) %reduce-scatter.12.cloned.1.call-update) | async-done | bytes 1048592 | tf_op jit(solution)/shard_map/reduce_scatter | solution.py:136
  1483.3 51.5 %all_to_all.189 = f32[1024,8,64]{0,2,1:T(8,128)S(1)} all-to-all(f32[1024,8,64]{0,2,1:T(8,128)S(1)} %bitcast.142), channel_id=1, replica_groups=mesh['elem'=8,'front'=4] {'elem'}, dimensions={1} | all-to-all | bytes 4194304 | tf_op jit(solution)/shard_map/all_to_all | solution.py:59
  1536.7 23.0 %collective-permute-done.24 = f32[4096,64]{0,1:T(8,128)S(1)} collective-permute-done((f32[4096,64]{0,1:T(8,128)S(1)}, f32[4096,64]{0,1:T(8,128)S(1)}, u32[]{:S(2)}, u32[]{:S(2)}) %collective-permute-start.24) | collective-permute-done | bytes 1048608 | tf_op jit(solution)/shard_map/ppermute | solution.py:11
  1572.7 30.1 %all_to_all.190 = bf16[8,1024,64]{1,2,0:T(8,128)(2,1)S(1)} all-to-all(bf16[8,1024,64]{1,2,0:T(8,128)(2,1)S(1)} %bitcast.137), channel_id=1, replica_groups=mesh['elem'=8,'front'=4] {'elem'}, dimensions={0} | all-to-all | bytes 2097152 | tf_op jit(solution)/shard_map/all_to_all | solution.py:55
  1618.5 167.2 %reduce-scatter.14.cloned.1.call-done = f32[8192,64]{0,1:T(8,128)} async-done(((f32[8192,512]{0,1:T(8,128)}), f32[8192,64]{0,1:T(8,128)}) %reduce-scatter.14.cloned.1.call-update) | async-done | bytes 2097168 | tf_op jit(solution)/shard_map/reduce_scatter | solution.py:136
  1787.6 16.0 collective-permute-done.26
  1803.6 16.0 collective-permute-done.27
  1819.6 16.0 collective-permute-done.28
  1835.7 16.0 collective-permute-done.29
  1851.7 16.0 collective-permute-done.30
  1867.7 16.0 collective-permute-done.31
  1883.9 16.0 collective-permute-done.32
  1931.3 51.6 %all_to_all.191 = f32[1024,8,64]{0,2,1:T(8,128)S(1)} all-to-all(f32[1024,8,64]{0,2,1:T(8,128)S(1)} %bitcast.140), channel_id=1, replica_groups=mesh['elem'=8,'front'=4] {'elem'}, dimensions={1} | all-to-all | bytes 4194304 | tf_op jit(solution)/shard_map/all_to_all | solution.py:59
  (218 shorter events, 424.5 us)
Async XLA Ops:
  6.5 137.4 %all-gather.8.cloned.1.call-start = ((), (), s32[]{:S(2)}) async-start(), calls=%async_computation.17 | async-start | bytes 1327104 | tf_op jit(solution)/shard_map/all_gather | solution.py:81
  12.6 143.3 %all-to-all-start = ((bf16[128,24,512]{0,1,2:T(8,128)(2,1)}), bf16[128,24,512]{0,1,2:T(8,128)(2,1)S(1)}, u32[]{:S(2)}, u32[]{:S(2)}) async-start(bf16[128,24,512]{0,1,2:T(8,128)(2,1)} %copy.36), calls=%async_computation | async-start | bytes 6291456 | tf_op jit(solution)/shard_map/all_to_all | solution.py:78
  19.0 129.5 %all-gather.6.cloned.1.call-start = ((), (), s32[]{:S(2)}) async-start(), calls=%async_computation.16 | async-start | bytes 1327104 | tf_op jit(solution)/shard_map/all_gather | solution.py:80
  19.7 505.4 %reduce-scatter.6.cloned.1.call-start = ((), (), s32[]{:S(2)}) async-start(), calls=%async_computation.18 | async-start | bytes 18874368 | tf_op jit(solution)/shard_map/reduce_scatter | solution.py:116
  358.0 250.5 %all-gather.10.cloned.1.call-start = ((), (), s32[]{:S(2)}) async-start(), calls=%async_computation.19 | async-start | bytes 9437184 | tf_op jit(solution)/shard_map/all_gather | solution.py:121
  624.3 53.5 %all-to-all-start.2 = ((f32[1024,8,64]{0,2,1:T(8,128)}), f32[1024,8,64]{0,2,1:T(8,128)}, u32[]{:S(2)}, u32[]{:S(2)}) async-start(f32[1024,8,64]{0,2,1:T(8,128)} %bitcast.138), calls=%async_computation.3 | async-start | bytes 4194304 | tf_op jit(solution)/shard_map/all_to_all | solution.py:59
  628.8 220.8 %reduce-scatter.8.cloned.1.call-start = ((), (), s32[]{:S(2)}) async-start(), calls=%async_computation.20 | async-start | bytes 9437184 | tf_op jit(solution)/shard_map/reduce_scatter | solution.py:116
  681.7 24.9 %collective-permute-start = (f32[4096,64]{0,1:T(8,128)}, f32[4096,64]{0,1:T(8,128)}, u32[]{:S(2)}, u32[]{:S(2)}) collective-permute-start(f32[4096,64]{0,1:T(8,128)} %bitcast.67), channel_id=1, source_target_pairs={{0,1},{1,0},{2,3},{3,2},{4,5},{5,4},{6,7},{7,6},{8,9},{9,8},{10,11... | collective-permute-start | bytes 3145736 | tf_op jit(solution)/shard_map/ppermute | solution.py:11
  708.1 12.6 collective-permute-start.1
  761.1 136.1 %all-gather.12.cloned.1.call-start = ((), (), s32[]{:S(2)}) async-start(), calls=%async_computation.21 | async-start | bytes 4718592 | tf_op jit(solution)/shard_map/all_gather | solution.py:121
  907.7 52.6 %all-to-all-start.4 = ((f32[1024,8,64]{0,2,1:T(8,128)}), f32[1024,8,64]{0,2,1:T(8,128)S(1)}, u32[]{:S(2)}, u32[]{:S(2)}) async-start(f32[1024,8,64]{0,2,1:T(8,128)} %bitcast.139), calls=%async_computation.6 | async-start | bytes 4194304 | tf_op jit(solution)/shard_map/all_to_all | solution.py:59
  911.3 191.9 %reduce-scatter.10.cloned.1.call-start = ((), (), s32[]{:S(2)}) async-start(), calls=%async_computation.22 | async-start | bytes 4718592 | tf_op jit(solution)/shard_map/reduce_scatter | solution.py:116
  960.6 24.7 %collective-permute-start.2 = (f32[4096,64]{0,1:T(8,128)S(1)}, f32[4096,64]{0,1:T(8,128)S(1)}, u32[]{:S(2)}, u32[]{:S(2)}) collective-permute-start(f32[4096,64]{0,1:T(8,128)S(1)} %bitcast.143), channel_id=1, source_target_pairs={{0,2},{1,3},{2,0},{3,1},{4,6},{5,7},{6,4},{7,5},{8,10},{9,11},{10,... | collective-permute-start | bytes 3145736 | tf_op jit(solution)/shard_map/ppermute | solution.py:11
  985.5 12.7 collective-permute-start.3
  1005.9 10.6 collective-permute-start.5
  1054.3 347.1 %reduce-scatter.12.cloned.1.call-start = ((), (), s32[]{:S(2)}) async-start(), calls=%async_computation.23 | async-start | bytes 9437184 | tf_op jit(solution)/shard_map/reduce_scatter | solution.py:136
  1216.0 24.6 %collective-permute-start.13 = (f32[4096,64]{0,1:T(8,128)S(1)}, f32[4096,64]{0,1:T(8,128)S(1)}, u32[]{:S(2)}, u32[]{:S(2)}) collective-permute-start(f32[4096,64]{0,1:T(8,128)S(1)} %bitcast.144), channel_id=1, source_target_pairs={{0,2},{1,3},{2,0},{3,1},{4,6},{5,7},{6,4},{7,5},{8,10},{9,11},{10,... | collective-permute-start | bytes 3145736 | tf_op jit(solution)/shard_map/ppermute | solution.py:11
  1240.8 12.5 collective-permute-start.14
  1260.7 10.5 collective-permute-start.16
  1312.8 472.9 %reduce-scatter.14.cloned.1.call-start = ((), (), s32[]{:S(2)}) async-start(), calls=%async_computation.24 | async-start | bytes 18874368 | tf_op jit(solution)/shard_map/reduce_scatter | solution.py:136
  1402.8 10.5 collective-permute-start.17
  1413.2 10.4 collective-permute-start.18
  1423.6 10.4 collective-permute-start.19
  1535.1 24.6 %collective-permute-start.24 = (f32[4096,64]{0,1:T(8,128)S(1)}, f32[4096,64]{0,1:T(8,128)S(1)}, u32[]{:S(2)}, u32[]{:S(2)}) collective-permute-start(f32[4096,64]{0,1:T(8,128)S(1)} %bitcast.145), channel_id=1, source_target_pairs={{0,1},{1,0},{2,3},{3,2},{4,5},{5,4},{6,7},{7,6},{8,9},{9,8},{10,11... | collective-permute-start | bytes 3145736 | tf_op jit(solution)/shard_map/ppermute | solution.py:11
  1559.9 12.5 collective-permute-start.25
  1787.5 16.1 collective-permute-start.26
  1803.6 16.0 collective-permute-start.27
  1819.6 16.0 collective-permute-start.28
  1835.7 16.0 collective-permute-start.29
  1851.7 16.0 collective-permute-start.30
  1867.7 16.0 collective-permute-start.31
  1883.7 16.2 collective-permute-start.32
  (23 other events, 966.5 us)
Sparse Core Ops, SparseCore 0:
  8.9 42.0 all-gather.7
  52.6 45.4 all-gather.5
  358.1 166.9 reduce-scatter.5
  528.0 80.4 all-gather.9
  761.2 88.3 reduce-scatter.7
  851.9 45.3 all-gather.11
  1054.4 48.7 reduce-scatter.9
  1313.0 88.3 reduce-scatter.11
  1618.6 167.0 reduce-scatter.13
